TPU v7x, 32 devices: a whole 2x2x4 slice. The times are simulated.
32 devices in a mesh: grp: 2 (over core), tile: 16 (over z, y, x).
Axes of the slice: x: 2, y: 2, z: 4, core: 2. Of those that a mesh axis runs over, the one named last changes fastest.
Arguments:
- source_points: float32 [2, 3, 524288], P('grp', None, 'tile'), may hold values from -6 to 6
- intersection: int32 [2, 2048, 1], P('grp', 'tile'), may hold values from 0 to 15; in each aligned block of 128 rows (0 to 127, 128 to 255, ..., all dimensions but the last counted through in order) at most 16 rows name the same one
- target_scan: int32 [2, 2048], P('grp', 'tile'), may hold values from 0 to 63
- matches: int32 [2, 524288], P('grp', 'tile'), may hold values from 0 to 511
- target_points: float32 [3, 524288], P(None, 'tile'), may hold values from -6 to 6
- target_normals: float32 [3, 524288], P(None, 'tile'), may hold values from -4 to 4
Outputs:
- pose_step: float32 [6, 1024], P(None, 'tile')
Inputs may be any that keep to these rules, and one draw needn't show every extreme that they name: `intersection`: within the blocks of one device (each aligned run of 128 rows), no index is named more than 16 times, a bound that some block reaches.
All inputs are finite; a program needn't handle non-finite values.
Results may differ from a plain program's by a relative error of at most 0.0003.
Values sent between devices are 32-bit elements; how exact they have to be, the bound alone decides.
No kernel may reach another device: no remote copies, remote signals or barrier semaphores. Data moves between devices by JAX's collectives and lax.ppermute only.
A program may use at most 64 MiB of HBM per device.

v0:
```python
import math

import jax
import jax.numpy as jnp
from jax import lax
from jax.sharding import PartitionSpec as P

SCANS_DEV = 64
TARGET_PTS = 512


DAMPING = 0.1
PRECISE = lax.Precision.HIGHEST


def cross_rows(first_vec, second_vec):
    return jnp.stack(
        [
            first_vec[1] * second_vec[2] - first_vec[2] * second_vec[1],
            first_vec[2] * second_vec[0] - first_vec[0] * second_vec[2],
            first_vec[0] * second_vec[1] - first_vec[1] * second_vec[0],
        ]
    )


def pair_terms(source, target, normal, usable):
    jacobian = (
        jnp.concatenate(
            [cross_rows(source, normal), normal, -cross_rows(target, normal), -normal], axis=0
        )
        * usable[None]
    )
    misfit = jnp.sum(normal * (source - target), axis=0) * usable
    normal_blocks = jnp.einsum("anks,bnks->abnk", jacobian, jacobian, precision=PRECISE)
    gradient = jnp.einsum("anks,nks->ank", jacobian, misfit, precision=PRECISE)
    layout = jacobian.shape[1:3]
    own_terms = jnp.concatenate(
        [normal_blocks[:6, :6].reshape((36,) + layout), gradient[:6]], axis=0
    )
    theirs = jnp.concatenate([normal_blocks[6:, 6:].reshape((36,) + layout), gradient[6:]], axis=0)
    return (own_terms, theirs)


def solve_poses(scan_totals):
    entries = [[scan_totals[6 * row_at + col_at] for col_at in range(6)] for row_at in range(6)]
    traced = entries[0][0]
    for step_at in range(1, 6):
        traced = traced + entries[step_at][step_at]
    shift_by = DAMPING * traced / 6.0
    for step_at in range(6):
        entries[step_at][step_at] = entries[step_at][step_at] + shift_by
    values = [-scan_totals[36 + row_at] for row_at in range(6)]
    for pivot_at in range(6):
        for row_at in range(pivot_at + 1, 6):
            factor = entries[row_at][pivot_at] / entries[pivot_at][pivot_at]
            for col_at in range(pivot_at, 6):
                entries[row_at][col_at] = (
                    entries[row_at][col_at] - factor * entries[pivot_at][col_at]
                )
            values[row_at] = values[row_at] - factor * values[pivot_at]
    result = [None] * 6
    for row_at in range(5, -1, -1):
        running = values[row_at]
        for col_at in range(row_at + 1, 6):
            running = running - entries[row_at][col_at] * result[col_at]
        result[row_at] = running / entries[row_at][row_at]
    return jnp.stack(result)


def body(source_points, intersection, target_scan, matches, target_points, target_normals):
    tile_count = lax.axis_size("tile")
    blocks = intersection.shape[1]
    capacity = 2 * blocks // tile_count
    slot_count = tile_count * capacity
    points = source_points.shape[2] // blocks
    per_scan = blocks // SCANS_DEV
    destin = intersection[0, :, 0]
    block_range = jnp.arange(blocks, dtype=jnp.int32)
    onehot_dest = (destin[:, None] == jnp.arange(tile_count, dtype=jnp.int32)[None, :]).astype(
        jnp.float32
    )
    lower = (block_range[:, None] >= block_range[None, :]).astype(jnp.float32)
    running = jnp.dot(lower, onehot_dest, precision=PRECISE)
    ranked = jnp.sum(running * onehot_dest, axis=1).astype(jnp.int32) - 1
    slot_of = destin * capacity + ranked
    placing = (slot_of[None, :] == jnp.arange(slot_count, dtype=jnp.int32)[:, None]).astype(
        jnp.float32
    )
    filled = jnp.sum(placing, axis=1) > 0.5
    safe_block = jnp.dot(placing, block_range.astype(jnp.float32), precision=PRECISE).astype(
        jnp.int32
    )
    shaped = (tile_count, capacity, points)
    coords = source_points[0].reshape(3, blocks, points)
    packed = jnp.einsum("sb,cbk->csk", placing, coords, precision=PRECISE).reshape((3,) + shaped)
    wanted = (target_scan[0][:, None] * TARGET_PTS + matches[0].reshape(blocks, points)).astype(
        jnp.float32
    )
    placed = jnp.dot(placing, wanted, precision=PRECISE).astype(jnp.int32)
    request = jnp.where(filled[:, None], placed, -1).reshape((1,) + shaped)
    tables = jnp.concatenate([target_points, target_normals], axis=0).reshape(
        6, SCANS_DEV, TARGET_PTS
    )
    tables = jnp.transpose(tables, (1, 0, 2)).reshape(SCANS_DEV, 6 * TARGET_PTS)
    scan_range = jnp.arange(SCANS_DEV, dtype=jnp.int32)
    column_range = jnp.arange(TARGET_PTS, dtype=jnp.int32)
    outgoing = jnp.concatenate([packed, request.astype(jnp.float32)], axis=0)
    incoming = lax.all_to_all(outgoing, "tile", split_axis=1, concat_axis=1, tiled=True)
    target_index = incoming[3:].astype(jnp.int32)
    lookup_target_index = target_index[0]
    outer = lookup_target_index.shape[:-1]
    width = lookup_target_index.shape[-1]
    items = math.prod(outer)
    flat = jnp.maximum(lookup_target_index, 0).reshape(items, width)
    item_scan = flat[:, 0] // TARGET_PTS
    within = flat % TARGET_PTS
    scan_pick = (item_scan[:, None] == scan_range[None, :]).astype(jnp.float32)
    block_tables = jnp.dot(scan_pick, tables, precision=PRECISE).reshape(items, 6, TARGET_PTS)
    group = math.gcd(items, 16)

    def select(pair):
        table_part, column_part = pair
        chooser = (column_part[:, None, :] == column_range[None, :, None]).astype(jnp.float32)
        return jnp.einsum("icj,ijk->ick", table_part, chooser, precision=PRECISE)

    picked = lax.map(
        select,
        (
            block_tables.reshape(items // group, group, 6, TARGET_PTS),
            within.reshape(items // group, group, width),
        ),
    )
    picked = jnp.transpose(picked.reshape(items, 6, width), (1, 0, 2)).reshape(
        (6,) + outer + (width,)
    )
    nearest = picked[:3]
    facing = picked[3:]
    usable = (target_index[0] >= 0).astype(jnp.float32)
    mine, far_terms = pair_terms(incoming[:3], nearest, facing, usable)
    returned = lax.all_to_all(mine, "tile", split_axis=1, concat_axis=1, tiled=True)
    leading = target_index[:, :, :, 0]
    owner_scan = jnp.where(leading >= 0, leading // TARGET_PTS, -1)
    source_scan = jnp.where(filled, safe_block // per_scan, -1)
    src_onehot = (source_scan[None, :] == scan_range[:, None]).astype(jnp.float32)
    tgt_onehot = (owner_scan.reshape(slot_count)[None, :] == scan_range[:, None]).astype(
        jnp.float32
    )
    local_sums = jnp.dot(returned.reshape(42, slot_count), src_onehot.T, precision=PRECISE)
    local_sums = local_sums + jnp.dot(
        far_terms.reshape(42, slot_count), tgt_onehot.T, precision=PRECISE
    )
    totals = lax.psum(local_sums, "grp")
    return solve_poses(totals)


def solution(mesh):
    in_specs = (
        P("grp", None, "tile"),
        P("grp", "tile", None),
        P("grp", "tile"),
        P("grp", "tile"),
        P(None, "tile"),
        P(None, "tile"),
    )
    out_specs = P(None, "tile")
    return jax.shard_map(body, mesh=mesh, in_specs=in_specs, out_specs=out_specs, check_vma=False)
```

profile of v0, /device:TPU:0, one launch (start us, length us, event | category | flops | bytes accessed | tf_op | source)
XLA Modules:
  0.0 147.4 jit_solution(17331304386599116131)
XLA Ops:
  2.5 1.9 %reduce.10 = s32[32768]{0:T(1024)S(1)} reduce(s32[1,32768]{1,0:T(1,128)} %param.11, s32[]{:T(128)} %broadcast.193), dimensions={0}, to_apply=%param.11.reduce_sub_computation.3 | reduce | bytes 262148 | tf_op args[3]
  5.1 2.1 %reduce = f32[3,32768]{1,0:T(4,128)S(1)} reduce(f32[1,3,32768]{2,0,1:T(1,128)} %param.8, f32[]{:T(128)} %constant.83), dimensions={0}, to_apply=%param.8.reduce_sub_computation | reduce | bytes 786436 | tf_op args[0]
  8.1 1.1 pad_maximum_fusion
  9.2 8.3 %all-to-all-start = ((f32[4,16,16,256]{3,2,0,1:T(8,128)}), f32[4,16,16,256]{3,2,0,1:T(8,128)S(1)}, u32[]{:S(2)}, u32[]{:S(2)}) async-start(f32[4,16,16,256]{3,2,0,1:T(8,128)} %pad_maximum_fusion), calls=%async_computation | async-start | bytes 2097152 | tf_op jit(solution)/shard_map/all_to_all | solution.py:108
  17.5 2.2 %pad_maximum_fusion.1 = f32[6,32768]{1,0:T(8,128)} fusion(f32[3,32768]{1,0:T(4,128)S(1)} %copy-done.2, f32[3,32768]{1,0:T(4,128)} %param.12), kind=kLoop, calls=%fused_computation.22 | loop fusion | flops 196608 | bytes 1572864 | tf_op jit(solution)/shard_map/concatenate | solution.py:101
  19.8 22.1 %all-to-all-done = f32[4,16,16,256]{3,2,0,1:T(8,128)S(1)} async-done(((f32[4,16,16,256]{3,2,0,1:T(8,128)}), f32[4,16,16,256]{3,2,0,1:T(8,128)S(1)}, u32[]{:S(2)}, u32[]{:S(2)}) %all-to-all-start) | async-done | bytes 1048608 | tf_op jit(solution)/shard_map/all_to_all | solution.py:108
  42.1 4.7 %fusion.15 = f32[16,16,6,512]{3,1,2,0:T(8,128)} fusion(s32[16,16]{1,0:T(8,128)S(1)} %eq.106, f32[8,8,6,512]{3,2,1,0:T(8,128)} %bitcast.126), kind=kOutput, calls=%fused_computation.24 | convolution fusion | flops 603996160 | bytes 3933184 | tf_op jit(solution)/shard_map/dot_general | solution.py:118
  47.0 60.6 %while.11 = (s32[]{:T(128)}, f32[16,16,6,256]{3,1,0,2:T(8,128)S(1)}, f32[16,16,6,512]{3,1,2,0:T(8,128)}, s32[16,16,256]{2,1,0:T(8,128)S(1)}, s32[]{:T(128)}) while((s32[]{:T(128)}, f32[16,16,6,256]{3,1,0,2:T(8,128)S(1)}, f32[16,16,6,512]{3,1,2,0:T(8,128)}, s32[16,16,256]{2,1,0:T(8,128)S(1)}, s32[]{:T(128)}) %tuple.70), condition=%wide.region_3.4_spmd.clone, body=%wide.region_2.3_spmd.clone.sunk | while | flops 153092096 | bytes 966729 | solution.py:126
  47.0 0.9 constant_dynamic-slice_fusion.2
  48.0 2.7 %fusion.107 = f32[1,16,6,256]{3,2,1,0:T(8,128)S(1)} fusion(s32[16,256]{1,0:T(8,128)S(1)} %dynamic-slice_bitcast_fusion.2, f32[1,16,6,512]{3,1,2,0:T(8,128)S(1)} %constant_dynamic-slice_fusion.2), kind=kOutput, calls=%fused_computation.4.clone.1 | convolution fusion | flops 153092096 | bytes 311296 | tf_op jit(solution)/shard_map/while/body/eval_jaxpr/icj,ijk->ick/dot_general | solution.py:124
  50.8 0.9 constant_dynamic-slice_fusion.2
  51.7 2.7 %fusion.107 = f32[1,16,6,256]{3,2,1,0:T(8,128)S(1)} fusion(s32[16,256]{1,0:T(8,128)S(1)} %dynamic-slice_bitcast_fusion.2, f32[1,16,6,512]{3,1,2,0:T(8,128)S(1)} %constant_dynamic-slice_fusion.2), kind=kOutput, calls=%fused_computation.4.clone.1 | convolution fusion | flops 153092096 | bytes 311296 | tf_op jit(solution)/shard_map/while/body/eval_jaxpr/icj,ijk->ick/dot_general | solution.py:124
  54.5 0.9 constant_dynamic-slice_fusion.2
  55.5 2.7 %fusion.107 = f32[1,16,6,256]{3,2,1,0:T(8,128)S(1)} fusion(s32[16,256]{1,0:T(8,128)S(1)} %dynamic-slice_bitcast_fusion.2, f32[1,16,6,512]{3,1,2,0:T(8,128)S(1)} %constant_dynamic-slice_fusion.2), kind=kOutput, calls=%fused_computation.4.clone.1 | convolution fusion | flops 153092096 | bytes 311296 | tf_op jit(solution)/shard_map/while/body/eval_jaxpr/icj,ijk->ick/dot_general | solution.py:124
  58.3 0.9 constant_dynamic-slice_fusion.2
  59.3 2.7 %fusion.107 = f32[1,16,6,256]{3,2,1,0:T(8,128)S(1)} fusion(s32[16,256]{1,0:T(8,128)S(1)} %dynamic-slice_bitcast_fusion.2, f32[1,16,6,512]{3,1,2,0:T(8,128)S(1)} %constant_dynamic-slice_fusion.2), kind=kOutput, calls=%fused_computation.4.clone.1 | convolution fusion | flops 153092096 | bytes 311296 | tf_op jit(solution)/shard_map/while/body/eval_jaxpr/icj,ijk->ick/dot_general | solution.py:124
  62.1 0.9 constant_dynamic-slice_fusion.2
  63.1 2.7 %fusion.107 = f32[1,16,6,256]{3,2,1,0:T(8,128)S(1)} fusion(s32[16,256]{1,0:T(8,128)S(1)} %dynamic-slice_bitcast_fusion.2, f32[1,16,6,512]{3,1,2,0:T(8,128)S(1)} %constant_dynamic-slice_fusion.2), kind=kOutput, calls=%fused_computation.4.clone.1 | convolution fusion | flops 153092096 | bytes 311296 | tf_op jit(solution)/shard_map/while/body/eval_jaxpr/icj,ijk->ick/dot_general | solution.py:124
  65.9 0.9 constant_dynamic-slice_fusion.2
  66.8 2.7 %fusion.107 = f32[1,16,6,256]{3,2,1,0:T(8,128)S(1)} fusion(s32[16,256]{1,0:T(8,128)S(1)} %dynamic-slice_bitcast_fusion.2, f32[1,16,6,512]{3,1,2,0:T(8,128)S(1)} %constant_dynamic-slice_fusion.2), kind=kOutput, calls=%fused_computation.4.clone.1 | convolution fusion | flops 153092096 | bytes 311296 | tf_op jit(solution)/shard_map/while/body/eval_jaxpr/icj,ijk->ick/dot_general | solution.py:124
  69.6 0.9 constant_dynamic-slice_fusion.2
  70.6 2.7 %fusion.107 = f32[1,16,6,256]{3,2,1,0:T(8,128)S(1)} fusion(s32[16,256]{1,0:T(8,128)S(1)} %dynamic-slice_bitcast_fusion.2, f32[1,16,6,512]{3,1,2,0:T(8,128)S(1)} %constant_dynamic-slice_fusion.2), kind=kOutput, calls=%fused_computation.4.clone.1 | convolution fusion | flops 153092096 | bytes 311296 | tf_op jit(solution)/shard_map/while/body/eval_jaxpr/icj,ijk->ick/dot_general | solution.py:124
  73.4 0.9 constant_dynamic-slice_fusion.2
  74.4 2.7 %fusion.107 = f32[1,16,6,256]{3,2,1,0:T(8,128)S(1)} fusion(s32[16,256]{1,0:T(8,128)S(1)} %dynamic-slice_bitcast_fusion.2, f32[1,16,6,512]{3,1,2,0:T(8,128)S(1)} %constant_dynamic-slice_fusion.2), kind=kOutput, calls=%fused_computation.4.clone.1 | convolution fusion | flops 153092096 | bytes 311296 | tf_op jit(solution)/shard_map/while/body/eval_jaxpr/icj,ijk->ick/dot_general | solution.py:124
  77.2 0.9 constant_dynamic-slice_fusion.2
  78.2 2.7 %fusion.107 = f32[1,16,6,256]{3,2,1,0:T(8,128)S(1)} fusion(s32[16,256]{1,0:T(8,128)S(1)} %dynamic-slice_bitcast_fusion.2, f32[1,16,6,512]{3,1,2,0:T(8,128)S(1)} %constant_dynamic-slice_fusion.2), kind=kOutput, calls=%fused_computation.4.clone.1 | convolution fusion | flops 153092096 | bytes 311296 | tf_op jit(solution)/shard_map/while/body/eval_jaxpr/icj,ijk->ick/dot_general | solution.py:124
  81.0 0.9 constant_dynamic-slice_fusion.2
  81.9 2.7 %fusion.107 = f32[1,16,6,256]{3,2,1,0:T(8,128)S(1)} fusion(s32[16,256]{1,0:T(8,128)S(1)} %dynamic-slice_bitcast_fusion.2, f32[1,16,6,512]{3,1,2,0:T(8,128)S(1)} %constant_dynamic-slice_fusion.2), kind=kOutput, calls=%fused_computation.4.clone.1 | convolution fusion | flops 153092096 | bytes 311296 | tf_op jit(solution)/shard_map/while/body/eval_jaxpr/icj,ijk->ick/dot_general | solution.py:124
  84.7 0.9 constant_dynamic-slice_fusion.2
  85.7 2.7 %fusion.107 = f32[1,16,6,256]{3,2,1,0:T(8,128)S(1)} fusion(s32[16,256]{1,0:T(8,128)S(1)} %dynamic-slice_bitcast_fusion.2, f32[1,16,6,512]{3,1,2,0:T(8,128)S(1)} %constant_dynamic-slice_fusion.2), kind=kOutput, calls=%fused_computation.4.clone.1 | convolution fusion | flops 153092096 | bytes 311296 | tf_op jit(solution)/shard_map/while/body/eval_jaxpr/icj,ijk->ick/dot_general | solution.py:124
  88.5 0.9 constant_dynamic-slice_fusion.2
  89.5 2.7 %fusion.107 = f32[1,16,6,256]{3,2,1,0:T(8,128)S(1)} fusion(s32[16,256]{1,0:T(8,128)S(1)} %dynamic-slice_bitcast_fusion.2, f32[1,16,6,512]{3,1,2,0:T(8,128)S(1)} %constant_dynamic-slice_fusion.2), kind=kOutput, calls=%fused_computation.4.clone.1 | convolution fusion | flops 153092096 | bytes 311296 | tf_op jit(solution)/shard_map/while/body/eval_jaxpr/icj,ijk->ick/dot_general | solution.py:124
  92.3 0.9 constant_dynamic-slice_fusion.2
  93.3 2.7 %fusion.107 = f32[1,16,6,256]{3,2,1,0:T(8,128)S(1)} fusion(s32[16,256]{1,0:T(8,128)S(1)} %dynamic-slice_bitcast_fusion.2, f32[1,16,6,512]{3,1,2,0:T(8,128)S(1)} %constant_dynamic-slice_fusion.2), kind=kOutput, calls=%fused_computation.4.clone.1 | convolution fusion | flops 153092096 | bytes 311296 | tf_op jit(solution)/shard_map/while/body/eval_jaxpr/icj,ijk->ick/dot_general | solution.py:124
  96.1 0.9 constant_dynamic-slice_fusion.2
  97.0 2.7 %fusion.107 = f32[1,16,6,256]{3,2,1,0:T(8,128)S(1)} fusion(s32[16,256]{1,0:T(8,128)S(1)} %dynamic-slice_bitcast_fusion.2, f32[1,16,6,512]{3,1,2,0:T(8,128)S(1)} %constant_dynamic-slice_fusion.2), kind=kOutput, calls=%fused_computation.4.clone.1 | convolution fusion | flops 153092096 | bytes 311296 | tf_op jit(solution)/shard_map/while/body/eval_jaxpr/icj,ijk->ick/dot_general | solution.py:124
  100.8 2.7 %fusion.107 = f32[1,16,6,256]{3,2,1,0:T(8,128)S(1)} fusion(s32[16,256]{1,0:T(8,128)S(1)} %dynamic-slice_bitcast_fusion.2, f32[1,16,6,512]{3,1,2,0:T(8,128)S(1)} %constant_dynamic-slice_fusion.2), kind=kOutput, calls=%fused_computation.4.clone.1 | convolution fusion | flops 153092096 | bytes 311296 | tf_op jit(solution)/shard_map/while/body/eval_jaxpr/icj,ijk->ick/dot_general | solution.py:124
  103.6 0.9 constant_dynamic-slice_fusion.2
  104.6 2.7 %fusion.107 = f32[1,16,6,256]{3,2,1,0:T(8,128)S(1)} fusion(s32[16,256]{1,0:T(8,128)S(1)} %dynamic-slice_bitcast_fusion.2, f32[1,16,6,512]{3,1,2,0:T(8,128)S(1)} %constant_dynamic-slice_fusion.2), kind=kOutput, calls=%fused_computation.4.clone.1 | convolution fusion | flops 153092096 | bytes 311296 | tf_op jit(solution)/shard_map/while/body/eval_jaxpr/icj,ijk->ick/dot_general | solution.py:124
  110.1 5.6 %fusion.9 = f32[12,12,16,16]{0,1,3,2:T(8,128)S(1)} fusion(f32[12,16,16,256]{3,2,1,0:T(8,128)S(1)} %broadcast_multiply_fusion), kind=kOutput, calls=%fused_computation.13 | convolution fusion | flops 113246208 | bytes 3293184 | tf_op jit(solution)/shard_map/anks,bnks->abnk/dot_general | solution.py:34
  115.8 1.7 %fusion.98 = (f32[6,6,16,16]{0,1,3,2:T(8,128)}, f32[6,6,16,16]{0,1,3,2:T(8,128)}) fusion(f32[12,12,16,16]{0,1,3,2:T(8,128)S(1)} %fusion.9), kind=kLoop, calls=%fused_computation.184 | loop fusion | bytes 147456 | tf_op jit(solution)/shard_map/slice | solution.py:40
  117.5 2.0 %copy.48 = f32[6,6,16,16]{3,2,1,0:T(8,128)S(1)} copy(f32[6,6,16,16]{0,1,3,2:T(8,128)} %get-tuple-element.108) | data formatting | bytes 73728 | tf_op jit(solution)/shard_map/slice | solution.py:38
  120.4 6.6 %fusion.5 = f32[16,16,1,12]{3,2,1,0:T(1,128)S(1)} fusion(f32[12,16,16,256]{3,2,1,0:T(8,128)S(1)} %broadcast_multiply_fusion, f32[16,16,256,1]{2,1,0,3:T(8,128)} %get-tuple-element.105), kind=kOutput, calls=%fused_computation.9 | convolution fusion | flops 9437184 | bytes 3420160 | tf_op jit(solution)/shard_map/anks,nks->ank/dot_general | solution.py:35
  128.0 5.9 %all-to-all-start.1 = ((f32[16,1,672]{2,1,0:T(1,128)}), f32[16,1,672]{2,1,0:T(1,128)S(1)}, u32[]{:S(2)}, u32[]{:S(2)}) async-start(f32[16,1,672]{2,1,0:T(1,128)} %reshape.337), calls=%async_computation.1 | async-start | bytes 98304 | tf_op jit(solution)/shard_map/all_to_all | solution.py:140
  133.8 1.0 slice_convert_fusion
  135.3 2.0 %copy.51 = f32[6,6,16,16]{3,2,1,0:T(8,128)S(1)} copy(f32[6,6,16,16]{0,1,3,2:T(8,128)} %get-tuple-element.107) | data formatting | bytes 73728 | tf_op jit(solution)/shard_map/slice | solution.py:40
  137.6 3.8 %all-to-all-done.1 = f32[16,1,672]{2,1,0:T(1,128)S(1)} async-done(((f32[16,1,672]{2,1,0:T(1,128)}), f32[16,1,672]{2,1,0:T(1,128)S(1)}, u32[]{:S(2)}, u32[]{:S(2)}) %all-to-all-start.1) | async-done | bytes 43040 | tf_op jit(solution)/shard_map/all_to_all | solution.py:140
  143.2 3.4 %psum.7 = f32[42,64]{1,0:T(8,128)S(1)} all-reduce(f32[42,64]{1,0:T(8,128)S(1)} %convolution_add_fusion), channel_id=1, replica_groups=mesh['grp'=2,'tile'=16] {'grp'}, use_global_device_ids=true, to_apply=%region_5.6 | all-reduce | flops 2688 | bytes 21504 | tf_op jit(solution)/shard_map/psum | solution.py:152
  (87 shorter events, 13.7 us)
Async XLA Ops:
  5.1 12.4 %copy-start.2 = (f32[3,32768]{1,0:T(4,128)S(1)}, f32[3,32768]{1,0:T(4,128)}, u32[]{:S(2)}) copy-start(f32[3,32768]{1,0:T(4,128)} %param.13) | copy-start | bytes 1179652
  9.2 32.7 %all-to-all-start = ((f32[4,16,16,256]{3,2,0,1:T(8,128)}), f32[4,16,16,256]{3,2,0,1:T(8,128)S(1)}, u32[]{:S(2)}, u32[]{:S(2)}) async-start(f32[4,16,16,256]{3,2,0,1:T(8,128)} %pad_maximum_fusion), calls=%async_computation | async-start | bytes 2097152 | tf_op jit(solution)/shard_map/all_to_all | solution.py:108
  41.9 67.0 %copy-start = (f32[4,16,16,256]{3,2,0,1:T(8,128)}, f32[4,16,16,256]{3,2,0,1:T(8,128)S(1)}, u32[]{:S(2)}) copy-start(f32[4,16,16,256]{3,2,0,1:T(8,128)S(1)} %all-to-all-done) | copy-start | bytes 3145732
  120.4 6.7 %copy-start.1 = (f32[36,16,16]{0,2,1:T(8,128)S(1)}, f32[36,16,16]{0,2,1:T(8,128)}, u32[]{:S(2)}) copy-start(f32[36,16,16]{0,2,1:T(8,128)} %copy.50) | copy-start | bytes 110596
  128.0 13.4 %all-to-all-start.1 = ((f32[16,1,672]{2,1,0:T(1,128)}), f32[16,1,672]{2,1,0:T(1,128)S(1)}, u32[]{:S(2)}, u32[]{:S(2)}) async-start(f32[16,1,672]{2,1,0:T(1,128)} %reshape.337), calls=%async_computation.1 | async-start | bytes 98304 | tf_op jit(solution)/shard_map/all_to_all | solution.py:140
where the time goes:
time: 148 us; the launch traced here: 147 us
  matrix products  63.2 us (43%)
  local copies, waits for them, and re-layouts  26.6 us (18%)
  waiting for transfers between devices  25.9 us (18%)
  starting transfers between devices  14.2 us (10%)
  other arithmetic  13 us (9%)
  blocking collectives  3.42 us (2%)
    dot_general x16, matrix products, select(): return jnp.einsum('icj,ijk->ick', table_part, chooser, precision=PRECISE)  43.9 us
    all_to_all x1, waiting for transfers between devices, body(): lax.all_to_all(outgoing, 'tile', split_axis=1, concat_axis=1, tiled=True)  22.1 us
    dynamic_slice x16, local copies, waits for them, and re-layouts, body(): lax.map(select, (block_tables.reshape(items // group, group, 6, TARGET_PT...  15.1 us
    all_to_all x1, starting transfers between devices, body(): lax.all_to_all(outgoing, 'tile', split_axis=1, concat_axis=1, tiled=True)  8.34 us
    dot_general x1, matrix products, pair_terms(): gradient = jnp.einsum('anks,nks->ank', jacobian, misfit, precision=PRECISE)  6.57 us
    all_to_all x1, starting transfers between devices, body(): lax.all_to_all(mine, 'tile', split_axis=1, concat_axis=1, tiled=True)  5.89 us
    dot_general x1, matrix products, pair_terms(): jnp.einsum('anks,bnks->abnk', jacobian, jacobian, precision=PRECISE)  5.64 us
    dot_general x1, matrix products, body(): jnp.dot(scan_pick, tables, precision=PRECISE).reshape(items, 6, TARGET_PTS)  4.73 us
  transfers between devices with their start and end apart: 2, of which 2 were waited for; matrix products, arithmetic and copies ran while one was open for 4% of the time, Pallas kernels for 0%

commit v1 on v0

v1 whole, which is shorter than its diff:
```python
import functools

import jax
import jax.numpy as jnp
from jax import lax
from jax.experimental import pallas as pl
from jax.experimental.pallas import tpu as pltpu
from jax.sharding import PartitionSpec as P

SCANS_DEV = 64
TARGET_PTS = 512
LANES = 128
GROUP = 8
HALF = 32

DAMPING = 0.1
PRECISE = lax.Precision.HIGHEST
PAIRS = [(r, c) for r in range(6) for c in range(r, 6)]
PAIR_AT = {pair: at for at, pair in enumerate(PAIRS)}


def pack_kernel(
    dest_ref, scan_ref, points_ref, matches_ref, out_ref, slot_scan_ref, count_ref, *, capacity, blocks, points
):
    tiles = count_ref.shape[0]
    halves = points // LANES
    slots = tiles * capacity
    per_scan = blocks // SCANS_DEV
    out_ref[...] = jnp.full(out_ref.shape, -1.0, jnp.float32)

    def clear_count(at, carry):
        count_ref[at] = 0
        return carry

    def clear_slot(at, carry):
        slot_scan_ref[at] = -1
        return carry

    lax.fori_loop(0, tiles, clear_count, 0, unroll=8)
    lax.fori_loop(0, slots, clear_slot, 0, unroll=8)

    def place(block, carry):
        dest = dest_ref[block]
        rank = count_ref[dest]
        count_ref[dest] = rank + 1
        slot = dest * capacity + rank
        slot_scan_ref[slot] = block // per_scan
        base = pl.multiple_of(slot * (4 * halves), 8)
        for half in range(halves):
            start = pl.multiple_of(block * points + half * LANES, LANES)
            span = pl.ds(start, LANES)
            out_ref[pl.ds(base + half * 4, 3), :] = points_ref[0, :, span]
            wanted = matches_ref[:, span] + scan_ref[block] * TARGET_PTS
            out_ref[pl.ds(base + half * 4 + 3, 1), :] = wanted.astype(jnp.float32)
        return carry

    lax.fori_loop(0, blocks, place, 0, unroll=4)


def cross(first, second):
    return [
        first[1] * second[2] - first[2] * second[1],
        first[2] * second[0] - first[0] * second[2],
        first[0] * second[1] - first[1] * second[0],
    ]


def pair_kernel(scan_ref, x_ref, table_ref, out_ref, picked_ref, *, points):
    groups = out_ref.shape[0] // GROUP
    halves = points // LANES
    chunks = TARGET_PTS // LANES
    lane = lax.broadcasted_iota(jnp.int32, (GROUP, LANES), 1)

    def one_group(group, carry):
        base = pl.multiple_of(group * (4 * halves * GROUP), 8)

        def field(comp):
            parts = [x_ref[pl.ds(base + 4 * half + comp, GROUP, stride=4 * halves), :] for half in range(halves)]
            return jnp.concatenate(parts, axis=1)

        def chosen(comp):
            parts = [picked_ref[pl.ds(half * 8 * GROUP + comp, GROUP, stride=8), :] for half in range(halves)]
            return jnp.concatenate(parts, axis=1)

        index = field(3).astype(jnp.int32)
        valid = index >= 0
        low = index & (LANES - 1)
        high = (index >> 7) & (chunks - 1)
        for item in range(GROUP):
            scan = jnp.maximum(scan_ref[group * GROUP + item], 0)
            start = pl.multiple_of(scan * TARGET_PTS, TARGET_PTS)
            parts = [
                table_ref[:, pl.ds(pl.multiple_of(start + at * LANES, LANES), LANES)] for at in range(chunks)
            ]
            for half in range(halves):
                span = slice(half * LANES, (half + 1) * LANES)
                low_at = jnp.broadcast_to(low[item : item + 1, span], (8, LANES))
                high_at = jnp.broadcast_to(high[item : item + 1, span], (8, LANES))
                found = jnp.take_along_axis(parts[0], low_at, axis=1, mode="promise_in_bounds")
                for at in range(1, chunks):
                    other = jnp.take_along_axis(parts[at], low_at, axis=1, mode="promise_in_bounds")
                    found = jnp.where(high_at == at, other, found)
                picked_ref[pl.ds((half * GROUP + item) * 8, 8), :] = found
        p = [field(comp) for comp in range(3)]
        q = [chosen(comp) for comp in range(3)]
        n = [jnp.where(valid, chosen(comp), 0.0) for comp in range(3, 6)]
        misfit = n[0] * (p[0] - q[0]) + n[1] * (p[1] - q[1]) + n[2] * (p[2] - q[2])
        own = cross(p, n) + n
        far = cross(q, n) + n

        def total(product):
            folded = product[:, :LANES]
            for half in range(1, halves):
                folded = folded + product[:, half * LANES : (half + 1) * LANES]
            return jnp.sum(folded, axis=1, keepdims=True)

        result = jnp.zeros((GROUP, LANES), jnp.float32)
        for at, (r, c) in enumerate(PAIRS):
            mine = total(own[r] * own[c])
            result = jnp.where(lane == at, mine, result)
            theirs = mine if r >= 3 else total(far[r] * far[c])
            result = jnp.where(lane == HALF + at, theirs, result)
        for at in range(6):
            mine = total(own[at] * misfit)
            result = jnp.where(lane == 21 + at, mine, result)
            theirs = mine if at >= 3 else total(far[at] * misfit)
            result = jnp.where(lane == HALF + 21 + at, -theirs, result)
        out_ref[pl.ds(pl.multiple_of(group * GROUP, GROUP), GROUP), :] = result
        return carry

    lax.fori_loop(0, groups, one_group, 0)


def solve_poses(totals):
    entries = [[totals[PAIR_AT[min(r, c), max(r, c)]] for c in range(6)] for r in range(6)]
    traced = entries[0][0]
    for at in range(1, 6):
        traced = traced + entries[at][at]
    shift_by = DAMPING * traced / 6.0
    for at in range(6):
        entries[at][at] = entries[at][at] + shift_by
    values = [-totals[21 + at] for at in range(6)]
    for pivot in range(6):
        for row in range(pivot + 1, 6):
            factor = entries[row][pivot] / entries[pivot][pivot]
            for col in range(pivot, 6):
                entries[row][col] = entries[row][col] - factor * entries[pivot][col]
            values[row] = values[row] - factor * values[pivot]
    result = [None] * 6
    for row in range(5, -1, -1):
        running = values[row]
        for col in range(row + 1, 6):
            running = running - entries[row][col] * result[col]
        result[row] = running / entries[row][row]
    return jnp.stack(result)


def body(source_points, intersection, target_scan, matches, target_points, target_normals):
    tiles = lax.axis_size("tile")
    blocks = intersection.shape[1]
    capacity = 2 * blocks // tiles
    slots = tiles * capacity
    points = source_points.shape[2] // blocks
    vmem = pl.BlockSpec(memory_space=pltpu.VMEM)
    smem = pl.BlockSpec(memory_space=pltpu.SMEM)
    message, slot_scan = pl.pallas_call(
        functools.partial(pack_kernel, capacity=capacity, blocks=blocks, points=points),
        out_shape=(
            jax.ShapeDtypeStruct((slots * 4 * points // LANES, LANES), jnp.float32),
            jax.ShapeDtypeStruct((slots,), jnp.int32),
        ),
        in_specs=[smem, smem, vmem, vmem],
        out_specs=(vmem, smem),
        scratch_shapes=[pltpu.SMEM((tiles,), jnp.int32)],
        name="pack",
    )(intersection.reshape(blocks), target_scan.reshape(blocks), source_points, matches)
    incoming = lax.all_to_all(message, "tile", split_axis=0, concat_axis=0, tiled=True)
    pad = jnp.zeros((2, target_points.shape[1]), jnp.float32)
    tables = jnp.concatenate([target_points, target_normals, pad], axis=0)
    leading = incoming.reshape(slots, 4 * points // LANES, LANES)[:, 3, 0].astype(jnp.int32)
    owner_scan = leading >> 9
    terms = pl.pallas_call(
        functools.partial(pair_kernel, points=points),
        out_shape=jax.ShapeDtypeStruct((slots, LANES), jnp.float32),
        in_specs=[smem, vmem, vmem],
        out_specs=vmem,
        scratch_shapes=[pltpu.VMEM((GROUP * 8 * points // LANES, LANES), jnp.float32)],
        name="pairs",
    )(owner_scan, incoming, tables)
    returned = lax.all_to_all(terms, "tile", split_axis=0, concat_axis=0, tiled=True)
    scans = jnp.arange(SCANS_DEV, dtype=jnp.int32)
    src_onehot = (slot_scan[:, None] == scans[None, :]).astype(jnp.float32)
    tgt_onehot = (owner_scan[:, None] == scans[None, :]).astype(jnp.float32)
    contract = (((0,), (0,)), ((), ()))
    far_sums = lax.dot_general(terms[:, HALF : 2 * HALF], tgt_onehot, contract, precision=PRECISE)
    sums = lax.dot_general(returned[:, :HALF], src_onehot, contract, precision=PRECISE) + far_sums
    totals = lax.psum(sums, "grp")
    return solve_poses(totals)


def solution(mesh):
    in_specs = (
        P("grp", None, "tile"),
        P("grp", "tile", None),
        P("grp", "tile"),
        P("grp", "tile"),
        P(None, "tile"),
        P(None, "tile"),
    )
    return jax.shard_map(body, mesh=mesh, in_specs=in_specs, out_specs=P(None, "tile"), check_vma=False)
```

time: 148 us -> 77.2 us (0.52)
  matrix products: 63.2 us -> 0.64 us
  local copies, waits for them, and re-layouts: 26.6 us -> 3.37 us
  Pallas kernels: 0 us -> 17.5 us
  blocking collectives: 3.42 us -> 17.2 us
  other arithmetic: 13 us -> 6.46 us
  starting transfers between devices: 14.2 us -> 8.48 us
  waiting for transfers between devices: 25.9 us -> 23.1 us
    dot_general x25 -> x2, matrix products: 63.2 us -> 0.64 us  [the longest x1 0.34 us: body(): lax.dot_general(terms[:, HALF:2 * HALF], tgt_onehot, contract, precision=...]
    pallas_call x0 -> x2, Pallas kernels: none -> 17.5 us  [the longest x1 13.4 us: body(): pl.pallas_call(functools.partial(pair_kernel, points=points), out_shape=j...]
    dynamic_slice x16 -> x0, local copies, waits for them, and re-layouts: 15.1 us -> none  [body(): lax.map(select, (block_tables.reshape(items // group, group, 6, TARGET_PT...]
    all_to_all x0 -> x1, blocking collectives: none -> 13.8 us  [body(): lax.all_to_all(terms, 'tile', split_axis=0, concat_axis=0, tiled=True)]
    slice x8 -> x0, local copies, waits for them, and re-layouts: 6.61 us -> none  [the longest x2 3.78 us: pair_terms(): normal_blocks[6:, 6:].reshape((36,) + layout)]
    all_to_all x2 -> x1, starting transfers between devices: 14.2 us -> 8.48 us  [body(): lax.all_to_all(message, 'tile', split_axis=0, concat_axis=0, tiled=True)]
    shift_right_arithmetic x0 -> x1, other arithmetic: none -> 5.14 us  [body(): owner_scan = leading >> 9]
    unnamed x6 -> x0, other arithmetic: 4.35 us -> none
  transfers between devices with their start and end apart: 2 -> 1, of which waited for: 2 -> 1; matrix products, arithmetic and copies ran while one was open for 4% -> 2% of each run, Pallas kernels for 0% -> 0%
where the time goes in v1:
time: 77.2 us; the launch traced here: 76.8 us
  waiting for transfers between devices  23.1 us (30%)
  Pallas kernels  17.5 us (23%)
  blocking collectives  17.2 us (22%)
  starting transfers between devices  8.48 us (11%)
  other arithmetic  6.46 us (8%)
  local copies, waits for them, and re-layouts  3.37 us (4%)
    all_to_all x1, waiting for transfers between devices, body(): lax.all_to_all(message, 'tile', split_axis=0, concat_axis=0, tiled=True)  23.1 us
    all_to_all x1, blocking collectives, body(): lax.all_to_all(terms, 'tile', split_axis=0, concat_axis=0, tiled=True)  13.8 us
    pallas_call x1, Pallas kernels, body(): pl.pallas_call(functools.partial(pair_kernel, points=points), out_shape=j...  13.4 us
    all_to_all x1, starting transfers between devices, body(): lax.all_to_all(message, 'tile', split_axis=0, concat_axis=0, tiled=True)  8.48 us
    shift_right_arithmetic x1, other arithmetic, body(): owner_scan = leading >> 9  5.14 us
    pallas_call x1, Pallas kernels, body(): pl.pallas_call(functools.partial(pack_kernel, capacity=capacity, blocks=b...  4.13 us
    psum x1, blocking collectives, body(): totals = lax.psum(sums, 'grp')  3.36 us
    unnamed x13, local copies, waits for them, and re-layouts  2.68 us
  transfers between devices with their start and end apart: 1, of which 1 were waited for; matrix products, arithmetic and copies ran while one was open for 2% of the time, Pallas kernels for 0%

profile of v1, /device:TPU:0, one launch (start us, length us, event | category | flops | bytes accessed | tf_op | source)
XLA Modules:
  0.0 76.8 jit_solution(14419550916376260870)
XLA Ops:
  0.0 2.1 %copy.9.points_ref = f32[1,3,32768]{2,1,0:T(4,128)} copy(f32[1,3,32768]{2,0,1:T(1,128)} %param.6) | data formatting | bytes 786432 | tf_op args[0]
  2.1 4.1 %pack.1 = (f32[2048,128]{1,0:T(8,128)}, s32[256]{0:T(256)}) custom-call(s32[128]{0:T(128)} %bitcast.12, s32[128]{0:T(128)} %bitcast.13, f32[1,3,32768]{2,1,0:T(4,128)} %copy.9.points_ref, s32[1,32768]{1,0:T(1,128)} %matches_ref.1), custom_call_target="tpu_custom_call" | custom-call | tf_op jit(solution)/shard_map/pack/pallas_call | solution.py:166
  6.2 0.0 copy-start.2
  6.2 0.0 copy-start.3
  6.2 8.5 %all-to-all-start = ((f32[16,128,128]{2,1,0:T(8,128)}), f32[16,128,128]{2,1,0:T(8,128)S(1)}, u32[]{:S(2)}, u32[]{:S(2)}) async-start(f32[16,128,128]{2,1,0:T(8,128)} %bitcast.10), calls=%async_computation | async-start | bytes 2097152 | tf_op jit(solution)/shard_map/all_to_all | solution.py:177
  14.7 0.1 pad.2.clone
  14.8 0.0 copy-done.2
  14.8 0.0 copy-done.3
  14.8 1.2 %maximum_maximum_fusion.table_ref = f32[8,32768]{1,0:T(8,128)} fusion(f32[3,32768]{1,0:T(4,128)S(1)} %copy-done.2, f32[3,32768]{1,0:T(4,128)S(1)} %copy-done.3, f32[8]{0:T(128)S(1)} %pad.2.clone), kind=kLoop, calls=%fused_computation.1 | loop fusion | flops 524288 | bytes 1835040 | tf_op jit(solution)/shard_map/concatenate | solution.py:179
  16.0 23.1 %all-to-all-done = f32[16,128,128]{2,1,0:T(8,128)S(1)} async-done(((f32[16,128,128]{2,1,0:T(8,128)}), f32[16,128,128]{2,1,0:T(8,128)S(1)}, u32[]{:S(2)}, u32[]{:S(2)}) %all-to-all-start) | async-done | bytes 1048608 | tf_op jit(solution)/shard_map/all_to_all | solution.py:177
  39.1 0.0 copy-start
  39.1 5.1 %fusion.4.scan_ref = s32[256]{0:T(256)} fusion(f32[256,8,128]{2,1,0:T(8,128)S(1)} %bitcast.7), kind=kLoop, calls=%fused_computation.9 | loop fusion | flops 512 | bytes 2048 | tf_op jit(solution)/shard_map/shift_right_arithmetic | solution.py:181
  44.2 0.0 copy-done
  44.2 13.4 %pairs.1 = f32[256,128]{1,0:T(8,128)} custom-call(s32[256]{0:T(256)} %fusion.4.scan_ref, f32[2048,128]{1,0:T(8,128)} %bitcast.8, f32[8,32768]{1,0:T(8,128)} %maximum_maximum_fusion.table_ref), custom_call_target="tpu_custom_call" | custom-call | tf_op jit(solution)/shard_map/pairs/pallas_call | solution.py:182
  57.6 0.0 copy-start.5
  57.6 13.8 %all_to_all.23 = f32[16,16,128]{2,1,0:T(8,128)S(1)} all-to-all(f32[16,16,128]{2,1,0:T(8,128)} %bitcast.9), channel_id=1, replica_groups=mesh['grp'=2,'tile'=16] {'tile'}, dimensions={0} | all-to-all | bytes 262144 | tf_op jit(solution)/shard_map/all_to_all | solution.py:190
  71.4 0.0 copy-start.1
  71.4 0.0 copy-done.5
  71.4 0.0 copy-start.4
  71.4 0.3 fusion.1
  71.7 0.6 copy-done.1
  72.3 0.0 copy-done.4
  72.3 0.3 convolution_add_fusion
  72.7 3.4 %psum.7 = f32[32,64]{1,0:T(8,128)S(1)} all-reduce(f32[32,64]{1,0:T(8,128)S(1)} %convolution_add_fusion), channel_id=1, replica_groups=mesh['grp'=2,'tile'=16] {'grp'}, use_global_device_ids=true, to_apply=%region_0.0 | all-reduce | flops 2048 | bytes 16384 | tf_op jit(solution)/shard_map/psum | solution.py:197
  76.1 0.1 subtract_divide_fusion
  76.2 0.6 stack.2
  (4 shorter events, 0.1 us)
Async XLA Ops:
  6.2 8.6 %copy-start.2 = (f32[3,32768]{1,0:T(4,128)S(1)}, f32[3,32768]{1,0:T(4,128)}, u32[]{:S(2)}) copy-start(f32[3,32768]{1,0:T(4,128)} %param.11) | copy-start | bytes 1179652
  6.2 8.6 %copy-start.3 = (f32[3,32768]{1,0:T(4,128)S(1)}, f32[3,32768]{1,0:T(4,128)}, u32[]{:S(2)}) copy-start(f32[3,32768]{1,0:T(4,128)} %param.10) | copy-start | bytes 1179652
  6.2 32.9 %all-to-all-start = ((f32[16,128,128]{2,1,0:T(8,128)}), f32[16,128,128]{2,1,0:T(8,128)S(1)}, u32[]{:S(2)}, u32[]{:S(2)}) async-start(f32[16,128,128]{2,1,0:T(8,128)} %bitcast.10), calls=%async_computation | async-start | bytes 2097152 | tf_op jit(solution)/shard_map/all_to_all | solution.py:177
  39.1 5.1 %copy-start = (f32[16,128,128]{2,1,0:T(8,128)}, f32[16,128,128]{2,1,0:T(8,128)S(1)}, u32[]{:S(2)}) copy-start(f32[16,128,128]{2,1,0:T(8,128)S(1)} %all-to-all-done) | copy-start | bytes 3145732
  57.6 13.8 %copy-start.5 = (s32[256]{0:T(256)S(1)}, s32[256]{0:T(256)}, u32[]{:S(2)}) copy-start(s32[256]{0:T(256)} %get-tuple-element.8) | copy-start | bytes 3076
  71.4 0.9 %copy-start.1 = (f32[256,128]{1,0:T(8,128)S(1)}, f32[256,128]{1,0:T(8,128)}, u32[]{:S(2)}) copy-start(f32[256,128]{1,0:T(8,128)} %pairs.1) | copy-start | bytes 393220
  71.4 0.9 %copy-start.4 = (s32[256]{0:T(256)S(1)}, s32[256]{0:T(256)}, u32[]{:S(2)}) copy-start(s32[256]{0:T(256)} %fusion.4.scan_ref) | copy-start | bytes 3076

commit v2 on v1

--- a/solution.py
+++ b/solution.py
@@ -1,4 +1,5 @@
 import functools
+import math
 
 import jax
 import jax.numpy as jnp
@@ -20,7 +21,7 @@
 
 
 def pack_kernel(
-    dest_ref, scan_ref, points_ref, matches_ref, out_ref, slot_scan_ref, count_ref, *, capacity, blocks, points
+    dest_ref, scan_ref, points_ref, matches_ref, out_ref, slot_scan_ref, count_ref, slot_ref, *, capacity, blocks, points
 ):
     tiles = count_ref.shape[0]
     halves = points // LANES
@@ -39,22 +40,36 @@
     lax.fori_loop(0, tiles, clear_count, 0, unroll=8)
     lax.fori_loop(0, slots, clear_slot, 0, unroll=8)
 
-    def place(block, carry):
+    def rank(block, carry):
         dest = dest_ref[block]
-        rank = count_ref[dest]
-        count_ref[dest] = rank + 1
-        slot = dest * capacity + rank
+        ranked = count_ref[dest]
+        count_ref[dest] = ranked + 1
+        slot = dest * capacity + ranked
         slot_scan_ref[slot] = block // per_scan
-        base = pl.multiple_of(slot * (4 * halves), 8)
-        for half in range(halves):
-            start = pl.multiple_of(block * points + half * LANES, LANES)
-            span = pl.ds(start, LANES)
-            out_ref[pl.ds(base + half * 4, 3), :] = points_ref[0, :, span]
-            wanted = matches_ref[:, span] + scan_ref[block] * TARGET_PTS
-            out_ref[pl.ds(base + half * 4 + 3, 1), :] = wanted.astype(jnp.float32)
-        return carry
-
-    lax.fori_loop(0, blocks, place, 0, unroll=4)
+        slot_ref[block] = slot
+        return carry
+
+    lax.fori_loop(0, blocks, rank, 0, unroll=4)
+    batch = 8
+
+    def place(step, carry):
+        loaded = []
+        for at in range(batch):
+            block = step * batch + at
+            offset = scan_ref[block] * TARGET_PTS
+            for half in range(halves):
+                span = pl.ds(pl.multiple_of(block * points + half * LANES, LANES), LANES)
+                wanted = matches_ref[:, span] + offset
+                loaded.append((points_ref[0, :, span], wanted.astype(jnp.float32)))
+        for at in range(batch):
+            base = pl.multiple_of(slot_ref[step * batch + at] * (4 * halves), 8)
+            for half in range(halves):
+                coords, wanted = loaded[at * halves + half]
+                out_ref[pl.ds(base + half * 4, 3), :] = coords
+                out_ref[pl.ds(base + half * 4 + 3, 1), :] = wanted
+        return carry
+
+    lax.fori_loop(0, blocks // batch, place, 0)
 
 
 def cross(first, second):
@@ -65,13 +80,37 @@
     ]
 
 
-def pair_kernel(scan_ref, x_ref, table_ref, out_ref, picked_ref, *, points):
-    groups = out_ref.shape[0] // GROUP
+def pair_kernel(x_ref, table_ref, own_ref, far_ref, owner_ref, all_ref, picked_ref, scan_ref, sem, *, points, fold):
+    slots = far_ref.shape[0]
+    groups = slots // GROUP
     halves = points // LANES
     chunks = TARGET_PTS // LANES
     lane = lax.broadcasted_iota(jnp.int32, (GROUP, LANES), 1)
 
-    def one_group(group, carry):
+    width = 4 * halves
+    for at in range(slots // LANES):
+        rows = x_ref[pl.ds(at * LANES * width + 3, LANES, stride=width), :]
+        owner_ref[at : at + 1, :] = rows.T[0:1, :].astype(jnp.int32) >> 9
+    copy = pltpu.make_async_copy(owner_ref, scan_ref, sem)
+    copy.start()
+    all_ref[...] = jnp.zeros(all_ref.shape, jnp.float32)
+    copy.wait()
+
+    def scan_at(item):
+        return scan_ref[item // LANES, item % LANES]
+
+    def maybe_group(group, carry):
+        used = scan_at(group * GROUP)
+        for item in range(1, GROUP):
+            used = jnp.maximum(used, scan_at(group * GROUP + item))
+
+        @pl.when(used >= 0)
+        def _():
+            one_group(group)
+
+        return carry
+
+    def one_group(group):
         base = pl.multiple_of(group * (4 * halves * GROUP), 8)
 
         def field(comp):
@@ -87,7 +126,7 @@
         low = index & (LANES - 1)
         high = (index >> 7) & (chunks - 1)
         for item in range(GROUP):
-            scan = jnp.maximum(scan_ref[group * GROUP + item], 0)
+            scan = jnp.maximum(scan_at(group * GROUP + item), 0)
             start = pl.multiple_of(scan * TARGET_PTS, TARGET_PTS)
             parts = [
                 table_ref[:, pl.ds(pl.multiple_of(start + at * LANES, LANES), LANES)] for at in range(chunks)
@@ -125,10 +164,17 @@
             result = jnp.where(lane == 21 + at, mine, result)
             theirs = mine if at >= 3 else total(far[at] * misfit)
             result = jnp.where(lane == HALF + 21 + at, -theirs, result)
-        out_ref[pl.ds(pl.multiple_of(group * GROUP, GROUP), GROUP), :] = result
-        return carry
-
-    lax.fori_loop(0, groups, one_group, 0)
+        all_ref[pl.ds(pl.multiple_of(group * GROUP, GROUP), GROUP), :] = result
+
+    lax.fori_loop(0, groups, maybe_group, 0)
+    far_ref[...] = all_ref[...]
+    rows = slots // fold
+    wide = lax.broadcasted_iota(jnp.int32, (rows, LANES), 1) // HALF
+    folded = all_ref[pl.ds(0, rows, stride=fold), :]
+    for at in range(1, fold):
+        moved = pltpu.roll(all_ref[pl.ds(at, rows, stride=fold), :], HALF * at, 1)
+        folded = jnp.where(wide == at, moved, folded)
+    own_ref[...] = folded
 
 
 def solve_poses(totals):
@@ -171,29 +217,40 @@
         ),
         in_specs=[smem, smem, vmem, vmem],
         out_specs=(vmem, smem),
-        scratch_shapes=[pltpu.SMEM((tiles,), jnp.int32)],
+        scratch_shapes=[pltpu.SMEM((tiles,), jnp.int32), pltpu.SMEM((blocks,), jnp.int32)],
         name="pack",
     )(intersection.reshape(blocks), target_scan.reshape(blocks), source_points, matches)
     incoming = lax.all_to_all(message, "tile", split_axis=0, concat_axis=0, tiled=True)
     pad = jnp.zeros((2, target_points.shape[1]), jnp.float32)
     tables = jnp.concatenate([target_points, target_normals, pad], axis=0)
-    leading = incoming.reshape(slots, 4 * points // LANES, LANES)[:, 3, 0].astype(jnp.int32)
-    owner_scan = leading >> 9
-    terms = pl.pallas_call(
-        functools.partial(pair_kernel, points=points),
-        out_shape=jax.ShapeDtypeStruct((slots, LANES), jnp.float32),
-        in_specs=[smem, vmem, vmem],
-        out_specs=vmem,
-        scratch_shapes=[pltpu.VMEM((GROUP * 8 * points // LANES, LANES), jnp.float32)],
+    fold = math.gcd(LANES // HALF, capacity)
+    mine, terms, owner_scan = pl.pallas_call(
+        functools.partial(pair_kernel, points=points, fold=fold),
+        out_shape=(
+            jax.ShapeDtypeStruct((slots // fold, LANES), jnp.float32),
+            jax.ShapeDtypeStruct((slots, LANES), jnp.float32),
+            jax.ShapeDtypeStruct((slots // LANES, LANES), jnp.int32),
+        ),
+        in_specs=[vmem, vmem],
+        out_specs=(vmem, vmem, vmem),
+        scratch_shapes=[
+            pltpu.VMEM((slots, LANES), jnp.float32),
+            pltpu.VMEM((GROUP * 8 * points // LANES, LANES), jnp.float32),
+            pltpu.SMEM((slots // LANES, LANES), jnp.int32),
+            pltpu.SemaphoreType.DMA,
+        ],
         name="pairs",
-    )(owner_scan, incoming, tables)
-    returned = lax.all_to_all(terms, "tile", split_axis=0, concat_axis=0, tiled=True)
+    )(incoming, tables)
+    returned = lax.all_to_all(mine, "tile", split_axis=0, concat_axis=0, tiled=True)
     scans = jnp.arange(SCANS_DEV, dtype=jnp.int32)
-    src_onehot = (slot_scan[:, None] == scans[None, :]).astype(jnp.float32)
-    tgt_onehot = (owner_scan[:, None] == scans[None, :]).astype(jnp.float32)
+    tgt_onehot = (owner_scan.reshape(slots)[:, None] == scans[None, :]).astype(jnp.float32)
     contract = (((0,), (0,)), ((), ()))
-    far_sums = lax.dot_general(terms[:, HALF : 2 * HALF], tgt_onehot, contract, precision=PRECISE)
-    sums = lax.dot_general(returned[:, :HALF], src_onehot, contract, precision=PRECISE) + far_sums
+    sums = lax.dot_general(terms[:, HALF : 2 * HALF], tgt_onehot, contract, precision=PRECISE)
+    places = slot_scan.reshape(slots // fold, fold)
+    for at in range(fold):
+        src_onehot = (places[:, at][:, None] == scans[None, :]).astype(jnp.float32)
+        part = returned[:, at * HALF : (at + 1) * HALF]
+        sums = sums + lax.dot_general(part, src_onehot, contract, precision=PRECISE)
     totals = lax.psum(sums, "grp")
     return solve_poses(totals)
 

time: 77.2 us -> 75.4 us (0.977)
  blocking collectives: 17.2 us -> 3.36 us
  starting transfers between devices: 8.48 us -> 17.1 us
  other arithmetic: 6.46 us -> 1.33 us
  waiting for transfers between devices: 23.1 us -> 27.6 us
  local copies, waits for them, and re-layouts: 3.37 us -> 5.45 us
  matrix products: 0.64 us -> 2.29 us
    all_to_all x1 -> x0, blocking collectives: 13.8 us -> none  [body(): lax.all_to_all(terms, 'tile', split_axis=0, concat_axis=0, tiled=True)]
    all_to_all x0 -> x1, starting transfers between devices: none -> 8.6 us  [body(): lax.all_to_all(mine, 'tile', split_axis=0, concat_axis=0, tiled=True)]
    all_to_all x0 -> x1, waiting for transfers between devices: none -> 5.48 us  [body(): lax.all_to_all(mine, 'tile', split_axis=0, concat_axis=0, tiled=True)]
    shift_right_arithmetic x1 -> x0, other arithmetic: 5.14 us -> none  [body(): owner_scan = leading >> 9]
    unnamed x13 -> x11, local copies, waits for them, and re-layouts: 2.68 us -> 4.43 us
    all_to_all x1, waiting for transfers between devices: 23.1 us -> 22.1 us  [body(): lax.all_to_all(message, 'tile', split_axis=0, concat_axis=0, tiled=True)]
    dot_general x1, matrix products: 0.34 us -> 1.24 us  [body(): lax.dot_general(terms[:, HALF:2 * HALF], tgt_onehot, contract, precision=...]
  transfers between devices with their start and end apart: 1 -> 2, of which waited for: 1 -> 2; matrix products, arithmetic and copies ran while one was open for 2% -> 4% of each run, Pallas kernels for 0% -> 0%
where the time goes in v2:
time: 75.4 us; the launch traced here: 75 us
  waiting for transfers between devices  27.6 us (37%)
  Pallas kernels  17.8 us (24%)
  starting transfers between devices  17.1 us (23%)
  local copies, waits for them, and re-layouts  5.45 us (7%)
  blocking collectives  3.36 us (4%)
  matrix products  2.29 us (3%)
  other arithmetic  1.33 us (2%)
    all_to_all x1, waiting for transfers between devices, body(): lax.all_to_all(message, 'tile', split_axis=0, concat_axis=0, tiled=True)  22.1 us
    pallas_call x1, Pallas kernels, body(): pl.pallas_call(functools.partial(pair_kernel, points=points, fold=fold),...  13.4 us
    all_to_all x1, starting transfers between devices, body(): lax.all_to_all(mine, 'tile', split_axis=0, concat_axis=0, tiled=True)  8.6 us
    all_to_all x1, starting transfers between devices, body(): lax.all_to_all(message, 'tile', split_axis=0, concat_axis=0, tiled=True)  8.48 us
    all_to_all x1, waiting for transfers between devices, body(): lax.all_to_all(mine, 'tile', split_axis=0, concat_axis=0, tiled=True)  5.48 us
    unnamed x11, local copies, waits for them, and re-layouts  4.43 us
    pallas_call x1, Pallas kernels, body(): pl.pallas_call(functools.partial(pack_kernel, capacity=capacity, blocks=b...  4.4 us
    psum x1, blocking collectives, body(): totals = lax.psum(sums, 'grp')  3.36 us
  transfers between devices with their start and end apart: 2, of which 2 were waited for; matrix products, arithmetic and copies ran while one was open for 4% of the time, Pallas kernels for 0%

profile of v2, /device:TPU:0, one launch (start us, length us, event | category | flops | bytes accessed | tf_op | source)
XLA Modules:
  0.0 75.0 jit_solution(15605892376316297753)
XLA Ops:
  0.0 2.0 %copy.9.points_ref = f32[1,3,32768]{2,1,0:T(4,128)} copy(f32[1,3,32768]{2,0,1:T(1,128)} %param.6) | data formatting | bytes 786432 | tf_op args[0]
  2.0 4.4 %pack.1 = (f32[2048,128]{1,0:T(8,128)}, s32[256]{0:T(256)}) custom-call(s32[128]{0:T(128)} %bitcast.15, s32[128]{0:T(128)} %bitcast.16, f32[1,3,32768]{2,1,0:T(4,128)} %copy.9.points_ref, s32[1,32768]{1,0:T(1,128)} %matches_ref.1), custom_call_target="tpu_custom_call" | custom-call | tf_op jit(solution)/shard_map/pack/pallas_call | solution.py:212
  6.5 0.0 copy-start.1
  6.5 0.0 copy-start.2
  6.5 8.5 %all-to-all-start = ((f32[16,128,128]{2,1,0:T(8,128)}), f32[16,128,128]{2,1,0:T(8,128)S(1)}, u32[]{:S(2)}, u32[]{:S(2)}) async-start(f32[16,128,128]{2,1,0:T(8,128)} %bitcast.8), calls=%async_computation | async-start | bytes 2097152 | tf_op jit(solution)/shard_map/all_to_all | solution.py:223
  15.0 0.1 pad.2.clone
  15.1 0.0 copy-done.1
  15.1 0.0 copy-done.2
  15.1 1.2 %maximum_maximum_fusion.table_ref = f32[8,32768]{1,0:T(8,128)} fusion(f32[3,32768]{1,0:T(4,128)S(1)} %copy-done.1, f32[3,32768]{1,0:T(4,128)S(1)} %copy-done.2, f32[8]{0:T(128)S(1)} %pad.2.clone), kind=kLoop, calls=%fused_computation.4 | loop fusion | flops 524288 | bytes 1835040 | tf_op jit(solution)/shard_map/concatenate | solution.py:225
  16.3 0.0 copy-start.4
  16.3 0.7 copy-done.4
  16.9 0.1 reshape.16
  17.1 0.2 slice_reduce_fusion
  17.3 22.1 %all-to-all-done = f32[16,128,128]{2,1,0:T(8,128)S(1)} async-done(((f32[16,128,128]{2,1,0:T(8,128)}), f32[16,128,128]{2,1,0:T(8,128)S(1)}, u32[]{:S(2)}, u32[]{:S(2)}) %all-to-all-start) | async-done | bytes 1048608 | tf_op jit(solution)/shard_map/all_to_all | solution.py:223
  39.4 0.0 copy-start
  39.4 1.0 %copy-done = f32[16,128,128]{2,1,0:T(8,128)} copy-done((f32[16,128,128]{2,1,0:T(8,128)}, f32[16,128,128]{2,1,0:T(8,128)S(1)}, u32[]{:S(2)}) %copy-start) | copy-done | bytes 1048600
  40.4 13.4 %pairs.1 = (f32[64,128]{1,0:T(8,128)}, f32[256,128]{1,0:T(8,128)}, s32[2,128]{1,0:T(2,128)}) custom-call(f32[2048,128]{1,0:T(8,128)} %bitcast.7, f32[8,32768]{1,0:T(8,128)} %maximum_maximum_fusion.table_ref), custom_call_target="tpu_custom_call" | custom-call | tf_op jit(solution)/shard_map/pairs/pallas_call | solution.py:227
  53.8 8.6 %all-to-all-start.1 = ((f32[16,4,128]{2,1,0:T(4,128)}), f32[16,4,128]{2,1,0:T(4,128)S(1)}, u32[]{:S(2)}, u32[]{:S(2)}) async-start(f32[16,4,128]{2,1,0:T(4,128)} %bitcast.13), calls=%async_computation.1 | async-start | bytes 65536 | tf_op jit(solution)/shard_map/all_to_all | solution.py:244
  62.4 0.0 copy-start.3
  62.4 0.7 copy-done.3
  63.1 1.2 %fusion = f32[32,64]{1,0:T(8,128)S(1)} fusion(f32[256,128]{1,0:T(8,128)} %get-tuple-element.11, s32[256]{0:T(256)S(1)} %bitcast.14), kind=kOutput, calls=%fused_computation.6 | convolution fusion | flops 6307840 | bytes 140288 | tf_op jit(solution)/shard_map/dot_general | solution.py:248
  64.3 5.5 %all-to-all-done.1 = f32[16,4,128]{2,1,0:T(4,128)S(1)} async-done(((f32[16,4,128]{2,1,0:T(4,128)}), f32[16,4,128]{2,1,0:T(4,128)S(1)}, u32[]{:S(2)}, u32[]{:S(2)}) %all-to-all-start.1) | async-done | bytes 32800 | tf_op jit(solution)/shard_map/all_to_all | solution.py:244
  69.8 0.2 convolution_add_fusion.3
  70.0 0.3 convolution_add_fusion.2
  70.3 0.3 convolution_add_fusion.1
  70.6 0.3 convolution_add_fusion
  70.9 3.4 %psum.7 = f32[32,64]{1,0:T(8,128)S(1)} all-reduce(f32[32,64]{1,0:T(8,128)S(1)} %convolution_add_fusion), channel_id=1, replica_groups=mesh['grp'=2,'tile'=16] {'grp'}, use_global_device_ids=true, to_apply=%region_0.0 | all-reduce | flops 2048 | bytes 16384 | tf_op jit(solution)/shard_map/psum | solution.py:254
  74.3 0.1 subtract_divide_fusion
  74.4 0.6 stack.2
  (4 shorter events, 0.1 us)
Async XLA Ops:
  6.5 8.6 %copy-start.1 = (f32[3,32768]{1,0:T(4,128)S(1)}, f32[3,32768]{1,0:T(4,128)}, u32[]{:S(2)}) copy-start(f32[3,32768]{1,0:T(4,128)} %param.11) | copy-start | bytes 1179652
  6.5 8.6 %copy-start.2 = (f32[3,32768]{1,0:T(4,128)S(1)}, f32[3,32768]{1,0:T(4,128)}, u32[]{:S(2)}) copy-start(f32[3,32768]{1,0:T(4,128)} %param.10) | copy-start | bytes 1179652
  6.5 32.9 %all-to-all-start = ((f32[16,128,128]{2,1,0:T(8,128)}), f32[16,128,128]{2,1,0:T(8,128)S(1)}, u32[]{:S(2)}, u32[]{:S(2)}) async-start(f32[16,128,128]{2,1,0:T(8,128)} %bitcast.8), calls=%async_computation | async-start | bytes 2097152 | tf_op jit(solution)/shard_map/all_to_all | solution.py:223
  16.3 0.7 copy-start.4
  39.4 1.0 %copy-start = (f32[16,128,128]{2,1,0:T(8,128)}, f32[16,128,128]{2,1,0:T(8,128)S(1)}, u32[]{:S(2)}) copy-start(f32[16,128,128]{2,1,0:T(8,128)S(1)} %all-to-all-done) | copy-start | bytes 3145732
  53.8 16.0 %all-to-all-start.1 = ((f32[16,4,128]{2,1,0:T(4,128)}), f32[16,4,128]{2,1,0:T(4,128)S(1)}, u32[]{:S(2)}, u32[]{:S(2)}) async-start(f32[16,4,128]{2,1,0:T(4,128)} %bitcast.13), calls=%async_computation.1 | async-start | bytes 65536 | tf_op jit(solution)/shard_map/all_to_all | solution.py:244
  62.4 0.7 copy-start.3

commit v3 on v2

--- a/solution.py
+++ b/solution.py
@@ -80,7 +80,7 @@
     ]
 
 
-def pair_kernel(x_ref, table_ref, own_ref, far_ref, owner_ref, all_ref, picked_ref, scan_ref, sem, *, points, fold):
+def pair_kernel(x_ref, table_ref, own_ref, far_ref, owner_ref, all_ref, picked_ref, scan_ref, list_ref, sem, *, points, fold):
     slots = far_ref.shape[0]
     groups = slots // GROUP
     halves = points // LANES
@@ -99,18 +99,16 @@
     def scan_at(item):
         return scan_ref[item // LANES, item % LANES]
 
-    def maybe_group(group, carry):
+    def list_group(group, count):
         used = scan_at(group * GROUP)
         for item in range(1, GROUP):
             used = jnp.maximum(used, scan_at(group * GROUP + item))
-
-        @pl.when(used >= 0)
-        def _():
-            one_group(group)
-
-        return carry
-
-    def one_group(group):
+        list_ref[count] = group
+        list_ref[count + 1] = group
+        return count + jnp.where(used >= 0, 1, 0)
+
+    def one_group(group, lane_of):
+        picked_at = lane_of * halves * 8 * GROUP
         base = pl.multiple_of(group * (4 * halves * GROUP), 8)
 
         def field(comp):
@@ -118,7 +116,7 @@
             return jnp.concatenate(parts, axis=1)
 
         def chosen(comp):
-            parts = [picked_ref[pl.ds(half * 8 * GROUP + comp, GROUP, stride=8), :] for half in range(halves)]
+            parts = [picked_ref[pl.ds(picked_at + half * 8 * GROUP + comp, GROUP, stride=8), :] for half in range(halves)]
             return jnp.concatenate(parts, axis=1)
 
         index = field(3).astype(jnp.int32)
@@ -139,7 +137,7 @@
                 for at in range(1, chunks):
                     other = jnp.take_along_axis(parts[at], low_at, axis=1, mode="promise_in_bounds")
                     found = jnp.where(high_at == at, other, found)
-                picked_ref[pl.ds((half * GROUP + item) * 8, 8), :] = found
+                picked_ref[pl.ds(picked_at + (half * GROUP + item) * 8, 8), :] = found
         p = [field(comp) for comp in range(3)]
         q = [chosen(comp) for comp in range(3)]
         n = [jnp.where(valid, chosen(comp), 0.0) for comp in range(3, 6)]
@@ -164,9 +162,17 @@
             result = jnp.where(lane == 21 + at, mine, result)
             theirs = mine if at >= 3 else total(far[at] * misfit)
             result = jnp.where(lane == HALF + 21 + at, -theirs, result)
-        all_ref[pl.ds(pl.multiple_of(group * GROUP, GROUP), GROUP), :] = result
-
-    lax.fori_loop(0, groups, maybe_group, 0)
+        return result
+
+    def two_groups(at, carry):
+        pair = [list_ref[2 * at], list_ref[jnp.minimum(2 * at + 1, count - 1)]]
+        results = [one_group(group, lane_of) for lane_of, group in enumerate(pair)]
+        for group, result in zip(pair, results):
+            all_ref[pl.ds(pl.multiple_of(group * GROUP, GROUP), GROUP), :] = result
+        return carry
+
+    count = lax.fori_loop(0, groups, list_group, 0)
+    lax.fori_loop(0, (count + 1) // 2, two_groups, 0)
     far_ref[...] = all_ref[...]
     rows = slots // fold
     wide = lax.broadcasted_iota(jnp.int32, (rows, LANES), 1) // HALF
@@ -235,8 +241,9 @@
         out_specs=(vmem, vmem, vmem),
         scratch_shapes=[
             pltpu.VMEM((slots, LANES), jnp.float32),
-            pltpu.VMEM((GROUP * 8 * points // LANES, LANES), jnp.float32),
+            pltpu.VMEM((2 * GROUP * 8 * points // LANES, LANES), jnp.float32),
             pltpu.SMEM((slots // LANES, LANES), jnp.int32),
+            pltpu.SMEM((slots // GROUP + 2,), jnp.int32),
             pltpu.SemaphoreType.DMA,
         ],
         name="pairs",
@@ -247,10 +254,10 @@
     contract = (((0,), (0,)), ((), ()))
     sums = lax.dot_general(terms[:, HALF : 2 * HALF], tgt_onehot, contract, precision=PRECISE)
     places = slot_scan.reshape(slots // fold, fold)
+    onehot = (places[:, :, None] == scans[None, None, :]).astype(jnp.float32)
+    spread = lax.dot_general(returned, onehot.reshape(-1, fold * SCANS_DEV), contract, precision=PRECISE)
     for at in range(fold):
-        src_onehot = (places[:, at][:, None] == scans[None, :]).astype(jnp.float32)
-        part = returned[:, at * HALF : (at + 1) * HALF]
-        sums = sums + lax.dot_general(part, src_onehot, contract, precision=PRECISE)
+        sums = sums + spread[at * HALF : (at + 1) * HALF, at * SCANS_DEV : (at + 1) * SCANS_DEV]
     totals = lax.psum(sums, "grp")
     return solve_poses(totals)
 

time: 75.4 us -> 74.6 us (0.989)
  Pallas kernels: 17.8 us -> 14.6 us
  starting transfers between devices: 17.1 us -> 19.6 us
  waiting for transfers between devices: 27.6 us -> 29.4 us
  matrix products: 2.29 us -> 0.62 us
    pallas_call x1, Pallas kernels: 13.4 us -> 10.2 us  [body(): pl.pallas_call(functools.partial(pair_kernel, points=points, fold=fold),...]
    all_to_all x1, starting transfers between devices: 8.6 us -> 11.1 us  [body(): lax.all_to_all(mine, 'tile', split_axis=0, concat_axis=0, tiled=True)]
    all_to_all x1, waiting for transfers between devices: 5.48 us -> 7.13 us  [body(): lax.all_to_all(mine, 'tile', split_axis=0, concat_axis=0, tiled=True)]
    dot_general x1, matrix products: 1.24 us -> 0.35 us  [body(): lax.dot_general(terms[:, HALF:2 * HALF], tgt_onehot, contract, precision=...]
    dot_general x4 -> x1, matrix products: 1.05 us -> 0.26 us  [body(): lax.dot_general(returned, onehot.reshape(-1, fold * SCANS_DEV), contract,...]
    unnamed x11 -> x13, local copies, waits for them, and re-layouts: 4.43 us -> 4.42 us
  transfers between devices with their start and end apart: 2 -> 2, of which waited for: 2 -> 2; matrix products, arithmetic and copies ran while one was open for 4% -> 2% of each run, Pallas kernels for 0% -> 0%
where the time goes in v3:
time: 74.6 us; the launch traced here: 74.5 us
  waiting for transfers between devices  29.4 us (39%)
  starting transfers between devices  19.6 us (26%)
  Pallas kernels  14.6 us (20%)
  local copies, waits for them, and re-layouts  5.34 us (7%)
  blocking collectives  3.36 us (5%)
  other arithmetic  1.46 us (2%)
    all_to_all x1, waiting for transfers between devices, body(): lax.all_to_all(message, 'tile', split_axis=0, concat_axis=0, tiled=True)  22.3 us
    all_to_all x1, starting transfers between devices, body(): lax.all_to_all(mine, 'tile', split_axis=0, concat_axis=0, tiled=True)  11.1 us
    pallas_call x1, Pallas kernels, body(): pl.pallas_call(functools.partial(pair_kernel, points=points, fold=fold),...  10.2 us
    all_to_all x1, starting transfers between devices, body(): lax.all_to_all(message, 'tile', split_axis=0, concat_axis=0, tiled=True)  8.48 us
    all_to_all x1, waiting for transfers between devices, body(): lax.all_to_all(mine, 'tile', split_axis=0, concat_axis=0, tiled=True)  7.13 us
    unnamed x13, local copies, waits for them, and re-layouts  4.42 us
    pallas_call x1, Pallas kernels, body(): pl.pallas_call(functools.partial(pack_kernel, capacity=capacity, blocks=b...  4.38 us
    psum x1, blocking collectives, body(): totals = lax.psum(sums, 'grp')  3.36 us
  transfers between devices with their start and end apart: 2, of which 2 were waited for; matrix products, arithmetic and copies ran while one was open for 2% of the time, Pallas kernels for 0%

profile of v3, /device:TPU:0, one launch (start us, length us, event | category | flops | bytes accessed | tf_op | source)
XLA Modules:
  0.0 74.5 jit_solution(10681669605434350000)
XLA Ops:
  0.0 2.1 %copy.8.points_ref = f32[1,3,32768]{2,1,0:T(4,128)} copy(f32[1,3,32768]{2,0,1:T(1,128)} %param.6) | data formatting | bytes 786432 | tf_op args[0]
  2.1 4.4 %pack.1 = (f32[2048,128]{1,0:T(8,128)}, s32[256]{0:T(256)}) custom-call(s32[128]{0:T(128)} %bitcast.14, s32[128]{0:T(128)} %bitcast.15, f32[1,3,32768]{2,1,0:T(4,128)} %copy.8.points_ref, s32[1,32768]{1,0:T(1,128)} %matches_ref.1), custom_call_target="tpu_custom_call" | custom-call | tf_op jit(solution)/shard_map/pack/pallas_call | solution.py:218
  6.4 0.0 copy-start.1
  6.5 0.0 copy-start.2
  6.5 8.5 %all-to-all-start = ((f32[16,128,128]{2,1,0:T(8,128)}), f32[16,128,128]{2,1,0:T(8,128)S(1)}, u32[]{:S(2)}, u32[]{:S(2)}) async-start(f32[16,128,128]{2,1,0:T(8,128)} %bitcast.10), calls=%async_computation | async-start | bytes 2097152 | tf_op jit(solution)/shard_map/all_to_all | solution.py:229
  15.0 0.1 pad.2.clone
  15.1 0.0 copy-done.1
  15.1 0.0 copy-done.2
  15.1 1.2 %maximum_maximum_fusion.table_ref = f32[8,32768]{1,0:T(8,128)} fusion(f32[3,32768]{1,0:T(4,128)S(1)} %copy-done.1, f32[3,32768]{1,0:T(4,128)S(1)} %copy-done.2, f32[8]{0:T(128)S(1)} %pad.2.clone), kind=kLoop, calls=%fused_computation.4 | loop fusion | flops 524288 | bytes 1835040 | tf_op jit(solution)/shard_map/concatenate | solution.py:231
  16.3 0.0 copy-start.5
  16.3 0.7 copy-done.5
  16.9 0.1 eq.44
  17.0 22.3 %all-to-all-done = f32[16,128,128]{2,1,0:T(8,128)S(1)} async-done(((f32[16,128,128]{2,1,0:T(8,128)}), f32[16,128,128]{2,1,0:T(8,128)S(1)}, u32[]{:S(2)}, u32[]{:S(2)}) %all-to-all-start) | async-done | bytes 1048608 | tf_op jit(solution)/shard_map/all_to_all | solution.py:229
  39.4 0.0 copy-start
  39.4 1.0 %copy-done = f32[16,128,128]{2,1,0:T(8,128)} copy-done((f32[16,128,128]{2,1,0:T(8,128)}, f32[16,128,128]{2,1,0:T(8,128)S(1)}, u32[]{:S(2)}) %copy-start) | copy-done | bytes 1048600
  40.4 10.2 %pairs.1 = (f32[64,128]{1,0:T(8,128)}, f32[256,128]{1,0:T(8,128)}, s32[2,128]{1,0:T(2,128)}) custom-call(f32[2048,128]{1,0:T(8,128)} %bitcast.9, f32[8,32768]{1,0:T(8,128)} %maximum_maximum_fusion.table_ref), custom_call_target="tpu_custom_call" | custom-call | tf_op jit(solution)/shard_map/pairs/pallas_call | solution.py:233
  50.6 11.1 %all-to-all-start.1 = ((f32[16,4,128]{2,1,0:T(4,128)}), f32[16,4,128]{2,1,0:T(4,128)S(1)}, u32[]{:S(2)}, u32[]{:S(2)}) async-start(f32[16,4,128]{2,1,0:T(4,128)} %bitcast.12), calls=%async_computation.1 | async-start | bytes 65536 | tf_op jit(solution)/shard_map/all_to_all | solution.py:251
  61.7 0.1 iota_compare_fusion
  61.8 0.0 copy-start.3
  61.8 0.1 eq.48
  61.9 7.1 %all-to-all-done.1 = f32[16,4,128]{2,1,0:T(4,128)S(1)} async-done(((f32[16,4,128]{2,1,0:T(4,128)}), f32[16,4,128]{2,1,0:T(4,128)S(1)}, u32[]{:S(2)}, u32[]{:S(2)}) %all-to-all-start.1) | async-done | bytes 32800 | tf_op jit(solution)/shard_map/all_to_all | solution.py:251
  69.1 0.3 fusion.16
  69.3 0.0 copy-start.4
  69.4 0.0 copy-done.3
  69.4 0.7 copy-done.4
  70.0 0.4 fusion.2
  70.4 3.4 %psum.7 = f32[32,64]{1,0:T(8,128)S(1)} all-reduce(f32[32,64]{1,0:T(8,128)S(1)} %fusion.2), channel_id=1, replica_groups=mesh['grp'=2,'tile'=16] {'grp'}, use_global_device_ids=true, to_apply=%region_0.0 | all-reduce | flops 2048 | bytes 16384 | tf_op jit(solution)/shard_map/psum | solution.py:261
  73.8 0.1 subtract_divide_fusion
  73.9 0.6 stack.2
  (4 shorter events, 0.1 us)
Async XLA Ops:
  6.4 8.6 %copy-start.1 = (f32[3,32768]{1,0:T(4,128)S(1)}, f32[3,32768]{1,0:T(4,128)}, u32[]{:S(2)}) copy-start(f32[3,32768]{1,0:T(4,128)} %param.11) | copy-start | bytes 1179652
  6.5 8.6 %copy-start.2 = (f32[3,32768]{1,0:T(4,128)S(1)}, f32[3,32768]{1,0:T(4,128)}, u32[]{:S(2)}) copy-start(f32[3,32768]{1,0:T(4,128)} %param.10) | copy-start | bytes 1179652
  6.5 32.9 %all-to-all-start = ((f32[16,128,128]{2,1,0:T(8,128)}), f32[16,128,128]{2,1,0:T(8,128)S(1)}, u32[]{:S(2)}, u32[]{:S(2)}) async-start(f32[16,128,128]{2,1,0:T(8,128)} %bitcast.10), calls=%async_computation | async-start | bytes 2097152 | tf_op jit(solution)/shard_map/all_to_all | solution.py:229
  16.3 0.7 copy-start.5
  39.4 1.0 %copy-start = (f32[16,128,128]{2,1,0:T(8,128)}, f32[16,128,128]{2,1,0:T(8,128)S(1)}, u32[]{:S(2)}) copy-start(f32[16,128,128]{2,1,0:T(8,128)S(1)} %all-to-all-done) | copy-start | bytes 3145732
  50.6 18.5 %all-to-all-start.1 = ((f32[16,4,128]{2,1,0:T(4,128)}), f32[16,4,128]{2,1,0:T(4,128)S(1)}, u32[]{:S(2)}, u32[]{:S(2)}) async-start(f32[16,4,128]{2,1,0:T(4,128)} %bitcast.12), calls=%async_computation.1 | async-start | bytes 65536 | tf_op jit(solution)/shard_map/all_to_all | solution.py:251
  61.8 7.5 %copy-start.3 = (f32[256,128]{1,0:T(8,128)S(1)}, f32[256,128]{1,0:T(8,128)}, u32[]{:S(2)}) copy-start(f32[256,128]{1,0:T(8,128)} %get-tuple-element.11) | copy-start | bytes 393220
  69.3 0.7 copy-start.4
